TPU v7x, 32 devices: a whole 2x2x4 slice. The times are simulated.
32 devices in a mesh: parts: 2 (over y), pool: 4 (over z), tp: 4 (over x, core).
Axes of the slice: x: 2, y: 2, z: 4, core: 2. Of those that a mesh axis runs over, the one named last changes fastest.
Arguments:
- queries: bfloat16 [4096, 8192], P(('parts', 'pool'), 'tp'), parts along dimension 0, may hold values from -400 to 400
- suffix_kv: bfloat16 [2, 8, 4096, 128], P(None, 'tp', ('parts', 'pool')), parts along dimension 2, may hold values from -12 to 12
- pool_kv: bfloat16 [2, 8, 64, 128, 128], P(None, 'tp', ('parts', 'pool')), parts along dimension 2, may hold values from -6 to 6
- prefix_pages: int32 [8], P('parts'), parts along dimension 0, may hold values from 1 to 4, as said below
- owner_start: int32 [8], P('parts'), parts along dimension 0, may hold values from 0 to 3
- page_slot: int32 [8, 4, 2], P('parts'), parts along dimension 0, may hold values from 0 to 7, as said below
Outputs:
- attention: bfloat16 [4096, 8192], P(('parts', 'pool'), 'tp'), parts along dimension 0
- new_pool: bfloat16 [2, 8, 64, 128, 128], P(None, 'tp', ('parts', 'pool')), parts along dimension 2
There are 2 independent parts, one for each index of `parts`. A program takes and returns all parts, laid end to end along the dimension named above; each array names one. Nothing has to cross between parts.
Inputs may be any that keep to these rules, and one draw needn't show every extreme that they name: For each owner o, the entries page_slot[:, o, :] name each of its 8 slots exactly once. `prefix_pages`: among the 4 requests of one serving group, at least one has exactly 4 prefix pages.
All inputs are finite; a program needn't handle non-finite values.
Results may differ from a plain program's by a relative error of at most 0.0035.
Values may be sent and summed in bfloat16 or wider, within the bound.
A program may use at most 128 MiB of HBM per device.

v0:
```python
import math

import jax
import jax.numpy as jnp
from jax import lax
from jax.sharding import PartitionSpec as P


def attend_block(running, query_heads, key_rows, value_rows, visible, score_scale):
    run_max, weight_sum, accumulated = running
    scores = (
        jnp.einsum("hgqd,hkd->hgqk", query_heads, key_rows, preferred_element_type=jnp.float32)
        * score_scale
    )
    scores = jnp.where(visible, scores, -jnp.inf)
    new_max = jnp.maximum(run_max, jnp.max(scores, axis=-1))
    factor = jnp.exp(run_max - new_max)
    weights = jnp.exp(scores - new_max[..., None])
    weight_sum = weight_sum * factor + jnp.sum(weights, axis=-1)
    accumulated = accumulated * factor[..., None] + jnp.einsum(
        "hgqk,hkd->hgqd",
        weights.astype(jnp.bfloat16),
        value_rows,
        preferred_element_type=jnp.float32,
    )
    return (new_max, weight_sum, accumulated)


def attend_pages(running, query_heads, received, numbers, length, score_scale):
    page_count = received.shape[2]
    page_len = received.shape[3]
    per_block = min(page_count, max(1, 512 // page_len))
    while page_count % per_block:
        per_block = per_block - 1

    def block_step(block_index, carried):
        block_start = block_index * per_block
        block_pages = lax.dynamic_slice_in_dim(received, block_start, per_block, 2)
        key_rows = block_pages[0].reshape(
            block_pages.shape[1], per_block * page_len, block_pages.shape[4]
        )
        value_rows = block_pages[1].reshape(
            block_pages.shape[1], per_block * page_len, block_pages.shape[4]
        )
        live_pages = lax.dynamic_slice_in_dim(numbers, block_start, per_block, 0) < length
        visible = jnp.repeat(live_pages, page_len)
        return attend_block(carried, query_heads, key_rows, value_rows, visible, score_scale)

    return lax.fori_loop(0, page_count // per_block, block_step, running)


def body(queries, suffix_kv, pool_kv, prefix_pages, owner_start, page_slot):
    groups = lax.axis_size("pool")
    my_index = lax.axis_index("pool")
    local_heads = pool_kv.shape[1]
    slot_count = pool_kv.shape[2]
    page_len = pool_kv.shape[3]
    head_dim = pool_kv.shape[4]
    levels = page_slot.shape[2]
    suffix = queries.shape[0]
    per_kv = queries.shape[1] // (local_heads * head_dim)
    suffix_pages = suffix // page_len
    score_scale = 1.0 / math.sqrt(head_dim)
    length = prefix_pages[my_index]
    start_owner = owner_start[my_index]
    owners = jnp.arange(groups, dtype=jnp.int32)
    my_slots = page_slot[:, my_index, :]

    def level_rows(begin_level, end_level):
        chosen = my_slots[:, begin_level:end_level].reshape(-1)
        return jnp.take(pool_kv, chosen, axis=2)

    def numbers_of(begin_level, end_level):
        within = jnp.mod(owners - start_owner, groups)
        level_ids = jnp.arange(begin_level, end_level, dtype=jnp.int32)
        return (level_ids[None, :] * groups + within[:, None]).reshape(-1)

    own_pages = suffix_kv.reshape(2, local_heads, suffix_pages, page_len, head_dim)
    offset = jnp.mod(owners - start_owner - length, groups)
    wanted = offset < suffix_pages
    picked = jnp.take(own_pages, jnp.minimum(offset, suffix_pages - 1), axis=2)
    back_send = jnp.where(wanted[None, None, :, None, None], picked, jnp.zeros_like(picked))
    level_spans = [(level_one, level_one + 1) for level_one in range(levels)]
    first_send = level_rows(level_spans[0][0], level_spans[0][1])
    first_recv = lax.all_to_all(first_send, "pool", split_axis=2, concat_axis=2, tiled=True)
    returned = lax.all_to_all(back_send, "pool", split_axis=2, concat_axis=2, tiled=True)
    query_heads = jnp.transpose(
        queries.reshape(suffix, local_heads, per_kv, head_dim), (1, 2, 0, 3)
    )
    causal = lax.broadcasted_iota(jnp.int32, (suffix, suffix), 1) <= lax.broadcasted_iota(
        jnp.int32, (suffix, suffix), 0
    )
    running = (
        jnp.full((local_heads, per_kv, suffix), -jnp.inf, jnp.float32),
        jnp.zeros((local_heads, per_kv, suffix), jnp.float32),
        jnp.zeros((local_heads, per_kv, suffix, head_dim), jnp.float32),
    )
    running = attend_block(running, query_heads, suffix_kv[0], suffix_kv[1], causal, score_scale)
    running = attend_pages(
        running,
        query_heads,
        first_recv,
        numbers_of(level_spans[0][0], level_spans[0][1]),
        length,
        score_scale,
    )
    for begin_level, end_level in level_spans[1:]:
        later_recv = lax.all_to_all(
            level_rows(begin_level, end_level), "pool", split_axis=2, concat_axis=2, tiled=True
        )
        running = attend_pages(
            running,
            query_heads,
            later_recv,
            numbers_of(begin_level, end_level),
            length,
            score_scale,
        )
    run_max, weight_sum, accumulated = running
    result = accumulated / weight_sum[..., None]
    result = (
        jnp.transpose(result, (2, 0, 1, 3))
        .reshape(suffix, local_heads * per_kv * head_dim)
        .astype(jnp.bfloat16)
    )
    offset_in = jnp.mod(my_index - owner_start - prefix_pages, groups)
    usable = offset_in < suffix_pages
    level_ids = jnp.minimum((prefix_pages + offset_in) // groups, levels - 1)
    target = jnp.take_along_axis(my_slots, level_ids[:, None], axis=1)[:, 0]
    target = jnp.where(usable, target, slot_count)
    new_pool = pool_kv.at[:, :, target].set(returned, mode="drop")
    return (result, new_pool)


def solution(mesh):
    in_specs = (
        P(("parts", "pool"), "tp"),
        P(None, "tp", ("parts", "pool"), None),
        P(None, "tp", ("parts", "pool"), None, None),
        P("parts"),
        P("parts"),
        P("parts", None, None),
    )
    out_specs = (P(("parts", "pool"), "tp"), P(None, "tp", ("parts", "pool"), None, None))
    return jax.shard_map(body, mesh=mesh, in_specs=in_specs, out_specs=out_specs, check_vma=False)
```

profile of v0, /device:TPU:0, one launch (start us, length us, event | category | flops | bytes accessed | tf_op | source)
XLA Modules:
  0.0 122.8 jit_solution(5285862944854950834)
XLA Ops:
  0.6 1.2 %copy.61 = bf16[2,2,8,128,128]{4,3,2,1,0:T(8,128)(2,1)S(1)} copy(bf16[2,2,8,128,128]{4,3,2,1,0:T(8,128)(2,1)} %param.10) | data formatting | bytes 2097152
  3.6 6.3 %all-to-all-start = ((bf16[2,2,4,128,128]{4,3,1,0,2:T(8,128)(2,1)}), bf16[2,2,4,128,128]{4,3,1,0,2:T(8,128)(2,1)}, u32[]{:S(2)}, u32[]{:S(2)}) async-start(bf16[2,2,4,128,128]{4,3,1,0,2:T(8,128)(2,1)} %select_bitcast_fusion.1), calls=%async_computation | async-start | bytes 1048576 | tf_op jit(solution)/shard_map/all_to_all | solution.py:85
  10.0 1.3 %dynamic_slice.17 = s32[1]{0:T(128)} dynamic-slice(s32[4]{0:T(128)} %param.12, s32[]{:T(128)S(6)} %select_n.118), dynamic_slice_sizes={1} | dynamic-slice | bytes 12 | tf_op jit(solution)/shard_map/dynamic_slice | solution.py:65
  11.3 1.2 %dynamic_slice.18 = s32[1]{0:T(128)} dynamic-slice(s32[4]{0:T(128)} %param.11, s32[]{:T(128)S(6)} %select_n.118), dynamic_slice_sizes={1} | dynamic-slice | bytes 12 | tf_op jit(solution)/shard_map/dynamic_slice | solution.py:64
  13.2 1.2 fusion.50
  16.5 1.4 %gather_fusion.3 = bf16[4,2,2,128,128]{4,3,2,1,0:T(8,128)(2,1)} fusion(bf16[2,2,8,128,128]{4,3,2,1,0:T(8,128)(2,1)S(1)} %copy.61, s32[1024]{0:T(1024)S(1)} %pad_clamp_fusion.1), kind=kCustom, calls=%fused_computation.1.clone | custom fusion | bytes 1048592 | tf_op jit(solution)/shard_map/jit(_take)/gather | solution.py:71
  17.9 2.2 %copy.40 = bf16[64,8,16,128]{3,2,1,0:T(8,128)(2,1)S(1)} copy(bf16[64,8,16,128]{3,1,2,0:T(8,128)(2,1)} %bitcast.169) | data formatting | bytes 4194304
  20.1 2.5 %gather_fusion = bf16[4,2,2,128,128]{4,3,2,1,0:T(8,128)(2,1)} fusion(bf16[2,2,4,128,128]{4,3,2,1,0:T(8,128)(2,1)} %bitcast.171, s32[1024]{0:T(1024)S(1)} %pad_clamp_fusion), kind=kCustom, calls=%fused_computation.2 | custom fusion | bytes 1048592 | tf_op jit(solution)/shard_map/jit(_take)/gather | solution.py:81
  22.6 1.9 %select_bitcast_fusion = bf16[2,2,4,128,128]{4,3,1,0,2:T(8,128)(2,1)} fusion(bf16[4,2,2,128,128]{4,3,2,1,0:T(8,128)(2,1)} %gather_fusion.3, pred[4]{0:T(512)(128)(4,1)S(1)} %get-tuple-element.77), kind=kLoop, calls=%fused_computation.45 | loop fusion | flops 262144 | bytes 1048580 | tf_op jit(solution)/shard_map/jit(_take)/select_n | solution.py:71
  24.6 8.3 %fusion.2 = (f32[2,8,512]{2,1,0:T(8,128)S(1)}, f32[2,8,512,512]{2,3,1,0:T(8,128)}) fusion(pred[512,512]{0,1:T(8,128)(4,1)S(1)} %iota_compare_fusion, bf16[2,2,512,128]{3,2,1,0:T(8,128)(2,1)} %param.9, bf16[512,2,8,128]{3,2,1,0:T(8,128)(2,1)S(1)} %bitcast.166), kind=kOutput, calls=%fused_computation.15 | convolution fusion | flops 1086316544 | bytes 19431424 | tf_op jit(solution)/shard_map/hgqd,hkd->hgqk/dot_general | solution.py:12
  32.8 9.4 %fusion.3 = f32[2,8,512]{2,1,0:T(8,128)S(1)} fusion(f32[2,8,512,512]{2,3,1,0:T(8,128)} %get-tuple-element.82, f32[2,8,512]{2,1,0:T(8,128)S(1)} %get-tuple-element.81, pred[512,512]{0,1:T(8,128)(4,1)S(1)} %iota_compare_fusion), kind=kLoop, calls=%fused_computation.16 | loop fusion | flops 16769024 | bytes 17104896 | tf_op jit(solution)/shard_map/reduce_sum | solution.py:19
  42.2 5.1 %all-to-all-start.1 = ((bf16[2,2,4,128,128]{4,3,1,0,2:T(8,128)(2,1)}), bf16[2,2,4,128,128]{4,3,1,0,2:T(8,128)(2,1)}, u32[]{:S(2)}, u32[]{:S(2)}) async-start(bf16[2,2,4,128,128]{4,3,1,0,2:T(8,128)(2,1)} %select_bitcast_fusion), calls=%async_computation.1 | async-start | bytes 1048576 | tf_op jit(solution)/shard_map/all_to_all | solution.py:108
  47.4 1.2 compare_and_fusion.2
  48.6 2.0 %select_bitcast_fusion.2 = bf16[2,2,4,128,128]{4,3,1,0,2:T(8,128)(2,1)} fusion(bf16[4,2,2,128,128]{4,3,2,1,0:T(8,128)(2,1)} %gather_fusion, pred[4]{0:T(512)(128)(4,1)S(1)} %get-tuple-element.86, pred[4]{0:T(512)(128)(4,1)S(1)} %get-tuple-element.85), kind=kLoop, calls=%fused_computation.47 | loop fusion | flops 524288 | bytes 1048584 | tf_op jit(solution)/shard_map/jit(_where)/select_n | solution.py:82
  50.6 1.9 %fusion.60 = (bf16[1,2,4,128,128]{4,3,1,0,2:T(8,128)(2,1)}, bf16[1,2,4,128,128]{4,3,1,0,2:T(8,128)(2,1)}) fusion(bf16[2,2,4,128,128]{4,3,1,0,2:T(8,128)(2,1)} %all-to-all-done), kind=kLoop, calls=%fused_computation.119 | loop fusion | bytes 1048576 | tf_op jit(solution)/shard_map/while/body/eval_jaxpr/slice | solution.py:42
  52.4 1.8 %copy.24 = bf16[1,2,4,128,128]{3,2,4,1,0:T(4,128)(2,1)} copy(bf16[1,2,4,128,128]{4,3,1,0,2:T(8,128)(2,1)} %get-tuple-element.72) | data formatting | bytes 524288 | tf_op jit(solution)/shard_map/while/body/eval_jaxpr/slice | solution.py:42
  54.3 1.8 %reshape.240 = bf16[2,512,128,1]{1,2,0,3:T(8,128)(2,1)} reshape(bf16[1,2,4,128,128]{3,2,4,1,0:T(4,128)(2,1)} %copy.24) | data formatting | bytes 524288 | tf_op jit(solution)/shard_map/while/body/eval_jaxpr/reshape;while/body/eval_jaxpr/squeeze | solution.py:42
  56.0 1.7 %copy.23 = bf16[1,2,4,128,128]{4,3,2,1,0:T(8,128)(2,1)} copy(bf16[1,2,4,128,128]{4,3,1,0,2:T(8,128)(2,1)} %get-tuple-element.73) | data formatting | bytes 524288 | tf_op jit(solution)/shard_map/while/body/eval_jaxpr/slice | solution.py:39
  57.7 3.7 %all-to-all-done.1 = bf16[2,2,4,128,128]{4,3,1,0,2:T(8,128)(2,1)} async-done(((bf16[2,2,4,128,128]{4,3,1,0,2:T(8,128)(2,1)}), bf16[2,2,4,128,128]{4,3,1,0,2:T(8,128)(2,1)}, u32[]{:S(2)}, u32[]{:S(2)}) %all-to-all-start.1) | async-done | bytes 524320 | tf_op jit(solution)/shard_map/all_to_all | solution.py:108
  61.4 4.3 %all-to-all-start.2 = ((bf16[2,2,4,128,128]{4,3,1,0,2:T(8,128)(2,1)}), bf16[2,2,4,128,128]{4,3,1,0,2:T(8,128)(2,1)}, u32[]{:S(2)}, u32[]{:S(2)}) async-start(bf16[2,2,4,128,128]{4,3,1,0,2:T(8,128)(2,1)} %select_bitcast_fusion.2), calls=%async_computation.2 | async-start | bytes 1048576 | tf_op jit(solution)/shard_map/all_to_all | solution.py:86
  65.7 1.9 %fusion.61 = (bf16[1,2,4,128,128]{4,3,1,0,2:T(8,128)(2,1)}, bf16[1,2,4,128,128]{4,3,1,0,2:T(8,128)(2,1)}) fusion(bf16[2,2,4,128,128]{4,3,1,0,2:T(8,128)(2,1)} %all-to-all-done.1), kind=kLoop, calls=%fused_computation.120 | loop fusion | bytes 1048576 | tf_op jit(solution)/shard_map/while/body/eval_jaxpr/slice | solution.py:42
  67.6 1.8 %copy.27 = bf16[1,2,4,128,128]{3,2,4,1,0:T(4,128)(2,1)} copy(bf16[1,2,4,128,128]{4,3,1,0,2:T(8,128)(2,1)} %get-tuple-element.74) | data formatting | bytes 524288 | tf_op jit(solution)/shard_map/while/body/eval_jaxpr/slice | solution.py:42
  69.4 1.8 %reshape.242 = bf16[2,512,128,1]{1,2,0,3:T(8,128)(2,1)} reshape(bf16[1,2,4,128,128]{3,2,4,1,0:T(4,128)(2,1)} %copy.27) | data formatting | bytes 524288 | tf_op jit(solution)/shard_map/while/body/eval_jaxpr/reshape;while/body/eval_jaxpr/squeeze | solution.py:42
  72.2 7.7 %bitcast_reduce_fusion = (f32[2,8,512]{2,1,0:T(8,128)S(1)}, f32[2,512,8,512]{3,1,2,0:T(8,128)}) fusion(pred[512]{0:T(512)(128)(4,1)S(1)} %broadcast_bitcast_fusion, bf16[2,512,128,1]{2,1,3,0:T(8,128)(2,1)S(1)} %bitcast.173, bf16[512,2,8,128]{3,2,1,0:T(8,128)(2,1)S(1)} %bitcast.167), kind=kOutput, calls=%fused_computation.6 | convolution fusion | flops 1086316544 | bytes 19169792 | tf_op jit(solution)/shard_map/while/body/eval_jaxpr/hgqd,hkd->hgqk/dot_general | solution.py:12
  79.8 2.7 %bitcast_reduce_fusion.1 = (f32[2,8,512]{2,1,0:T(8,128)S(1)}, f32[2,512,8,512]{3,1,2,0:T(8,128)S(1)}) fusion(pred[512]{0:T(512)(128)(4,1)S(1)} %broadcast_bitcast_fusion.1, bf16[2,512,128,1]{2,1,3,0:T(8,128)(2,1)S(1)} %bitcast.172, bf16[512,2,8,128]{3,2,1,0:T(8,128)(2,1)S(1)} %bitcast.168), kind=kOutput, calls=%fused_computation.9 | convolution fusion | flops 1086316544 | bytes 19169792 | tf_op jit(solution)/shard_map/while/body/eval_jaxpr/hgqd,hkd->hgqk/dot_general | solution.py:12
  82.6 7.9 %fusion.7 = f32[2,8,512]{2,1,0:T(8,128)S(1)} fusion(f32[2,512,8,512]{3,1,2,0:T(8,128)} %get-tuple-element.80, f32[2,8,512]{2,1,0:T(8,128)S(1)} %get-tuple-element.57, pred[512]{0:T(512)(128)(4,1)S(1)} %broadcast_bitcast_fusion), kind=kLoop, calls=%fused_computation.20 | loop fusion | flops 16769024 | bytes 16843264 | tf_op jit(solution)/shard_map/while/body/eval_jaxpr/reduce_sum | solution.py:19
  90.5 8.0 %fusion.9 = f32[2,8,512,128]{2,3,1,0:T(8,128)S(1)} fusion(f32[2,512,8,512]{3,1,2,0:T(8,128)} %get-tuple-element.80, f32[2,8,512]{2,1,0:T(8,128)S(1)} %get-tuple-element.57, pred[512]{0:T(512)(128)(4,1)S(1)} %broadcast_bitcast_fusion, bf16[2,512,128,1]{1,2,0,3:T(8,128)(2,1)S(1)} %copy-done.6), kind=kOutput, calls=%fused_computation.22 | convolution fusion | flops 1090519040 | bytes 21266944 | tf_op jit(solution)/shard_map/while/body/eval_jaxpr/hgqk,hkd->hgqd/dot_general | solution.py:20
  98.5 3.8 %fusion.5 = f32[2,8,512]{2,1,0:T(8,128)S(1)} fusion(f32[2,512,8,512]{3,1,2,0:T(8,128)S(1)} %get-tuple-element.84, f32[2,8,512]{2,1,0:T(8,128)S(1)} %get-tuple-element.58, pred[512]{0:T(512)(128)(4,1)S(1)} %broadcast_bitcast_fusion.1), kind=kLoop, calls=%fused_computation.18 | loop fusion | flops 16769024 | bytes 16843264 | tf_op jit(solution)/shard_map/while/body/eval_jaxpr/reduce_sum | solution.py:19
  102.3 5.5 %fusion.11 = f32[2,8,512,128]{2,3,1,0:T(8,128)} fusion(f32[2,512,8,512]{3,1,2,0:T(8,128)S(1)} %get-tuple-element.84, f32[2,8,512]{2,1,0:T(8,128)S(1)} %get-tuple-element.58, pred[512]{0:T(512)(128)(4,1)S(1)} %broadcast_bitcast_fusion.1, bf16[2,512,128,1]{1,2,0,3:T(8,128)(2,1)S(1)} %copy-done.5), kind=kOutput, calls=%fused_computation.23 | convolution fusion | flops 1090519040 | bytes 21266944 | tf_op jit(solution)/shard_map/while/body/eval_jaxpr/hgqk,hkd->hgqd/dot_general | solution.py:20
  107.9 9.7 %fusion.19 = bf16[512,2,8,128]{0,3,2,1:T(8,128)(2,1)S(1)} fusion(f32[2,8,512,128]{2,3,1,0:T(8,128)S(1)} %fusion.9, f32[2,8,512,128]{2,3,1,0:T(8,128)} %fusion.11, f32[2,8,512,512]{2,3,1,0:T(8,128)} %get-tuple-element.82, f32[2,8,512]{2,1,0:T(8,128)S(1)} %get-tuple-element.81, pred[512,512]{0,1:T(8,128)(4,1)S(1)} %iota_compare_fusion, ...), kind=kOutput, calls=%fused_computation.30 | convolution fusion | flops 1097859072 | bytes 27951104 | tf_op jit(solution)/shard_map/hgqk,hkd->hgqd/dot_general | solution.py:20
  117.6 2.4 %copy.29 = bf16[512,2048]{1,0:T(8,128)(2,1)} copy(bf16[512,2048]{0,1:T(8,128)(2,1)S(1)} %bitcast.170) | data formatting | bytes 4194304
  120.0 1.8 %scatter_fusion = bf16[2,2,8,128,128]{4,3,2,1,0:T(8,128)(2,1)S(1)} fusion(bf16[2,2,8,128,128]{4,3,2,1,0:T(8,128)(2,1)S(1)} %copy.61, s32[4]{0:T(128)S(1)} %compare_select_fusion.4, bf16[4,2,2,128,128]{4,3,2,1,0:T(8,128)(2,1)} %bitcast.42), kind=kCustom, calls=%fused_computation.4 | custom fusion | bytes 1572880 | tf_op jit(solution)/shard_map/scatter | solution.py:131
  (37 shorter events, 6.6 us)
Async XLA Ops:
  0.6 1.3 %copy-start = (s32[4,4,2]{1,2,0:T(2,128)S(1)}, s32[4,4,2]{1,2,0:T(2,128)}, u32[]{:S(2)}) copy-start(s32[4,4,2]{1,2,0:T(2,128)} %param.13) | copy-start | bytes 388
  3.6 38.6 %all-to-all-start = ((bf16[2,2,4,128,128]{4,3,1,0,2:T(8,128)(2,1)}), bf16[2,2,4,128,128]{4,3,1,0,2:T(8,128)(2,1)}, u32[]{:S(2)}, u32[]{:S(2)}) async-start(bf16[2,2,4,128,128]{4,3,1,0,2:T(8,128)(2,1)} %select_bitcast_fusion.1), calls=%async_computation | async-start | bytes 1048576 | tf_op jit(solution)/shard_map/all_to_all | solution.py:85
  42.2 19.1 %all-to-all-start.1 = ((bf16[2,2,4,128,128]{4,3,1,0,2:T(8,128)(2,1)}), bf16[2,2,4,128,128]{4,3,1,0,2:T(8,128)(2,1)}, u32[]{:S(2)}, u32[]{:S(2)}) async-start(bf16[2,2,4,128,128]{4,3,1,0,2:T(8,128)(2,1)} %select_bitcast_fusion), calls=%async_computation.1 | async-start | bytes 1048576 | tf_op jit(solution)/shard_map/all_to_all | solution.py:108
  61.4 58.6 %all-to-all-start.2 = ((bf16[2,2,4,128,128]{4,3,1,0,2:T(8,128)(2,1)}), bf16[2,2,4,128,128]{4,3,1,0,2:T(8,128)(2,1)}, u32[]{:S(2)}, u32[]{:S(2)}) async-start(bf16[2,2,4,128,128]{4,3,1,0,2:T(8,128)(2,1)} %select_bitcast_fusion.2), calls=%async_computation.2 | async-start | bytes 1048576 | tf_op jit(solution)/shard_map/all_to_all | solution.py:86
  71.2 8.7 %copy-start.4 = (bf16[1,2,4,128,128]{4,3,2,1,0:T(8,128)(2,1)S(1)}, bf16[1,2,4,128,128]{4,3,2,1,0:T(8,128)(2,1)}, u32[]{:S(2)}) copy-start(bf16[1,2,4,128,128]{4,3,2,1,0:T(8,128)(2,1)} %copy.23) | copy-start | bytes 786436
  79.8 10.7 %copy-start.6 = (bf16[2,512,128,1]{1,2,0,3:T(8,128)(2,1)S(1)}, bf16[2,512,128,1]{1,2,0,3:T(8,128)(2,1)}, u32[]{:S(2)}) copy-start(bf16[2,512,128,1]{1,2,0,3:T(8,128)(2,1)} %reshape.242) | copy-start | bytes 786436
  90.5 11.8 %copy-start.5 = (bf16[2,512,128,1]{1,2,0,3:T(8,128)(2,1)S(1)}, bf16[2,512,128,1]{1,2,0,3:T(8,128)(2,1)}, u32[]{:S(2)}) copy-start(bf16[2,512,128,1]{1,2,0,3:T(8,128)(2,1)} %reshape.240) | copy-start | bytes 786436
  98.5 9.4 %copy-start.3 = (bf16[2,2,512,128]{3,2,1,0:T(8,128)(2,1)S(1)}, bf16[2,2,512,128]{3,2,1,0:T(8,128)(2,1)}, u32[]{:S(2)}) copy-start(bf16[2,2,512,128]{3,2,1,0:T(8,128)(2,1)} %param.9) | copy-start | bytes 1572868
  107.8 14.9 %copy-start.1 = (s32[4,4,2]{1,2,0:T(2,128)S(1)}, s32[4,4,2]{1,2,0:T(2,128)}, u32[]{:S(2)}) copy-start(s32[4,4,2]{1,2,0:T(2,128)} %param.13) | copy-start | bytes 388
  121.8 1.0 copy-start.2
where the time goes:
time: 124 us; the launch traced here: 123 us
  matrix products  41.8 us (34%)
  other arithmetic  30.5 us (25%)
  local copies, waits for them, and re-layouts  30.1 us (24%)
  starting transfers between devices  15.8 us (13%)
  waiting for transfers between devices  3.71 us (3%)
    dot_general x3, matrix products, attend_block(): jnp.einsum('hgqk,hkd->hgqd', weights.astype(jnp.bfloat16), value_rows, pr...  23.2 us
    reduce_sum x3, other arithmetic, attend_block(): weight_sum = weight_sum * factor + jnp.sum(weights, axis=-1)  21.1 us
    dot_general x3, matrix products, attend_block(): jnp.einsum('hgqd,hkd->hgqk', query_heads, key_rows, preferred_element_typ...  18.6 us
    slice x4, local copies, waits for them, and re-layouts, block_step(): block_pages[1]  7.37 us
    unnamed x18, local copies, waits for them, and re-layouts  6.81 us
    all_to_all x1, starting transfers between devices, body(): lax.all_to_all(first_send, 'pool', split_axis=2, concat_axis=2, tiled=True)  6.35 us
    all_to_all x1, starting transfers between devices, body(): lax.all_to_all(level_rows(begin_level, end_level), 'pool', split_axis=2,...  5.11 us
    all_to_all x1, starting transfers between devices, body(): lax.all_to_all(back_send, 'pool', split_axis=2, concat_axis=2, tiled=True)  4.32 us
  transfers between devices with their start and end apart: 3, of which 1 were waited for; matrix products, arithmetic and copies ran while one was open for 79% of the time, Pallas kernels for 0%

commit v1 on v0

v1 whole, which is shorter than its diff:
```python
import functools
import math

import jax
import jax.numpy as jnp
from jax import lax
from jax.experimental import pallas as pl
from jax.experimental.pallas import tpu as pltpu
from jax.sharding import PartitionSpec as P

NT = (((1,), (1,)), ((), ()))
ROWS = 128
KEY_BLOCK = 512


def kernel(
    groups,
    prefix_levels,
    length_ref,
    start_ref,
    slot_ref,
    q_ref,
    own_ref,
    pool_ref,
    out_ref,
    new_ref,
    send,
    recv,
    back_send,
    back_recv,
    own_values,
    page_keys,
    page_values,
    acc,
    top,
    send_sem,
    recv_sem,
    back_send_sem,
    back_recv_sem,
):
    me = lax.axis_index("pool")
    local_heads = pool_ref.shape[1]
    slot_count = pool_ref.shape[2]
    page_len = pool_ref.shape[3]
    dim = pool_ref.shape[4]
    levels = slot_ref.shape[1]
    suffix = q_ref.shape[0]
    heads = q_ref.shape[1] // dim
    per_kv = heads // local_heads
    suffix_pages = suffix // page_len
    factor = math.log2(math.e) / math.sqrt(dim)
    rows = min(ROWS, suffix)

    def wrap(value):
        return lax.rem(value + groups * (levels + 1), groups)

    barrier = pltpu.get_barrier_semaphore()
    for step in range(1, groups):
        pl.semaphore_signal(
            barrier,
            inc=1,
            device_id={"pool": lax.rem(me + step, groups)},
            device_id_type=pl.DeviceIdType.MESH,
        )

    my_start = start_ref[me]
    my_length = length_ref[me]
    for level in range(prefix_levels):
        for step in range(groups):
            request = lax.rem(me + step, groups)
            page = pool_ref[:, :, slot_ref[request, level, me]]
            if step:
                send[level * groups + step] = page
            else:
                recv[level * groups] = page
    for step in range(groups):
        offset = wrap(me + step - my_start - my_length)
        offset = jnp.minimum(offset, suffix_pages - 1)
        page = own_ref[:, :, offset]
        if step:
            back_send[step] = page
        else:
            back_recv[0] = page
    for head in range(local_heads):
        own_values[head, :, :dim] = own_ref[1, head].reshape(suffix, dim)
        own_values[head, :, dim:] = jnp.ones((suffix, dim), jnp.bfloat16)

    pl.semaphore_wait(barrier, groups - 1)
    copies = []
    back_copies = []
    for level in range(prefix_levels):
        for step in range(1, groups):
            place = level * groups + step
            copy = pltpu.make_async_remote_copy(
                src_ref=send.at[place],
                dst_ref=recv.at[place],
                send_sem=send_sem.at[place],
                recv_sem=recv_sem.at[place],
                device_id={"pool": lax.rem(me + step, groups)},
                device_id_type=pl.DeviceIdType.MESH,
            )
            copy.start()
            copies.append(copy)
    for step in range(1, groups):
        copy = pltpu.make_async_remote_copy(
            src_ref=back_send.at[step],
            dst_ref=back_recv.at[step],
            send_sem=back_send_sem.at[step],
            recv_sem=back_recv_sem.at[step],
            device_id={"pool": lax.rem(me + step, groups)},
            device_id_type=pl.DeviceIdType.MESH,
        )
        copy.start()
        back_copies.append(copy)

    causal = lax.broadcasted_iota(jnp.int32, (rows, rows), 1) <= lax.broadcasted_iota(
        jnp.int32, (rows, rows), 0
    )

    def own_step(head, carry):
        kv_head = head // per_kv
        columns = pl.ds(pl.multiple_of(head * dim, dim), dim)
        for first in range(0, suffix, rows):
            end = first + rows
            scores = lax.dot_general(
                q_ref[first:end, columns],
                own_ref[0, kv_head, : end // page_len].reshape(end, dim),
                NT,
                preferred_element_type=jnp.float32,
            )
            last = jnp.where(causal, scores[:, first:], -jnp.inf)
            scores = jnp.concatenate([scores[:, :first], last], axis=1) if first else last
            highest = jnp.max(scores, axis=1, keepdims=True)
            weights = jnp.exp2((scores - highest) * factor).astype(jnp.bfloat16)
            acc[head, first:end] = jnp.dot(
                weights, own_values[kv_head, :end], preferred_element_type=jnp.float32
            )
            top[head, first:end] = jnp.broadcast_to(highest, (rows, dim))
        return carry

    lax.fori_loop(0, heads, own_step, 0)

    for copy in copies:
        copy.wait()
    first_page = wrap(me - my_start)
    for level in range(prefix_levels):
        for step in range(groups):
            place = level * groups + step
            number = level * groups + wrap(me - step - my_start)
            live = number < my_length
            source = jnp.where(live, place, first_page)
            keep = live.astype(jnp.float32)
            span = slice(place * page_len, (place + 1) * page_len)
            for head in range(local_heads):
                page_keys[head, span] = recv[source, 0, head]
                page_values[head, span, :dim] = (
                    recv[place, 1, head].astype(jnp.float32) * keep
                ).astype(jnp.bfloat16)
                page_values[head, span, dim:] = jnp.full(
                    (page_len, dim), keep, jnp.float32
                ).astype(jnp.bfloat16)

    total = prefix_levels * groups * page_len
    block = min(KEY_BLOCK, total)

    def page_step(head, carry):
        kv_head = head // per_kv
        columns = pl.ds(pl.multiple_of(head * dim, dim), dim)
        for first in range(0, suffix, rows):
            end = first + rows
            mixed = acc[head, first:end]
            highest = top[head, first:end]
            for key_first in range(0, total, block):
                width = min(block, total - key_first)
                scores = lax.dot_general(
                    q_ref[first:end, columns],
                    page_keys[kv_head, key_first : key_first + width],
                    NT,
                    preferred_element_type=jnp.float32,
                )
                risen = jnp.maximum(highest, jnp.max(scores, axis=1, keepdims=True))
                shrink = jnp.exp2((highest - risen) * factor)
                weights = jnp.concatenate(
                    [
                        jnp.exp2((scores[:, at : at + dim] - risen) * factor).astype(jnp.bfloat16)
                        for at in range(0, width, dim)
                    ],
                    axis=1,
                )
                mixed = mixed * jnp.concatenate([shrink, shrink], axis=1) + jnp.dot(
                    weights,
                    page_values[kv_head, key_first : key_first + width],
                    preferred_element_type=jnp.float32,
                )
                highest = risen
            out_ref[first:end, columns] = (mixed[:, :dim] / mixed[:, dim:]).astype(jnp.bfloat16)
        return carry

    lax.fori_loop(0, heads, page_step, 0)

    for copy in back_copies:
        copy.wait()
    targets = []
    for step in range(groups):
        request = lax.rem(me - step + groups, groups)
        offset = wrap(me - start_ref[request] - length_ref[request])
        level = jnp.minimum((length_ref[request] + offset) // groups, levels - 1)
        target = slot_ref[request, level, me]
        targets.append(jnp.where(offset < suffix_pages, target, slot_count))

    def slot_step(slot, carry):
        chosen = jnp.int32(0)
        hit = jnp.int32(0)
        for step in range(groups):
            match = targets[step] == slot
            chosen = jnp.where(match, step, chosen)
            hit = jnp.where(match, 1, hit)
        taken = jnp.full((page_len, dim), hit, jnp.int32) > 0
        for which in range(2):
            for head in range(local_heads):
                fresh = back_recv[chosen, which, head].astype(jnp.float32)
                old = pool_ref[which, head, slot].astype(jnp.float32)
                new_ref[which, head, slot] = jnp.where(taken, fresh, old).astype(jnp.bfloat16)
        return carry

    lax.fori_loop(0, slot_count, slot_step, 0)


def body(queries, suffix_kv, pool_kv, prefix_pages, owner_start, page_slot):
    groups = lax.axis_size("pool")
    _, local_heads, slot_count, page_len, dim = pool_kv.shape
    levels = page_slot.shape[2]
    suffix, width = queries.shape
    heads = width // dim
    suffix_pages = suffix // page_len
    prefix_levels = max(1, -(-(groups * levels - suffix_pages) // groups))
    pages = prefix_levels * groups
    page_shape = (2, local_heads, page_len, dim)
    smem = pl.BlockSpec(memory_space=pltpu.SMEM)
    vmem = pl.BlockSpec(memory_space=pltpu.VMEM)
    bf16 = jnp.bfloat16
    return pl.pallas_call(
        functools.partial(kernel, groups, prefix_levels),
        out_shape=(
            jax.ShapeDtypeStruct(queries.shape, bf16),
            jax.ShapeDtypeStruct(pool_kv.shape, bf16),
        ),
        in_specs=[smem, smem, smem, vmem, vmem, vmem],
        out_specs=(vmem, vmem),
        scratch_shapes=[
            pltpu.VMEM((pages,) + page_shape, bf16),
            pltpu.VMEM((pages,) + page_shape, bf16),
            pltpu.VMEM((groups,) + page_shape, bf16),
            pltpu.VMEM((groups,) + page_shape, bf16),
            pltpu.VMEM((local_heads, suffix, 2 * dim), bf16),
            pltpu.VMEM((local_heads, pages * page_len, dim), bf16),
            pltpu.VMEM((local_heads, pages * page_len, 2 * dim), bf16),
            pltpu.VMEM((heads, suffix, 2 * dim), jnp.float32),
            pltpu.VMEM((heads, suffix, dim), jnp.float32),
            pltpu.SemaphoreType.DMA((pages,)),
            pltpu.SemaphoreType.DMA((pages,)),
            pltpu.SemaphoreType.DMA((groups,)),
            pltpu.SemaphoreType.DMA((groups,)),
        ],
        compiler_params=pltpu.CompilerParams(
            collective_id=0, has_side_effects=True, vmem_limit_bytes=56 * 1024 * 1024
        ),
    )(
        prefix_pages,
        owner_start,
        jnp.transpose(page_slot, (0, 2, 1)),
        queries,
        suffix_kv.reshape(2, local_heads, suffix_pages, page_len, dim),
        pool_kv,
    )


def solution(mesh):
    in_specs = (
        P(("parts", "pool"), "tp"),
        P(None, "tp", ("parts", "pool"), None),
        P(None, "tp", ("parts", "pool"), None, None),
        P("parts"),
        P("parts"),
        P("parts", None, None),
    )
    out_specs = (P(("parts", "pool"), "tp"), P(None, "tp", ("parts", "pool"), None, None))
    return jax.shard_map(body, mesh=mesh, in_specs=in_specs, out_specs=out_specs, check_vma=False)
```

time: 124 us -> 44.4 us (0.36)
  matrix products: 41.8 us -> 0 us
  Pallas kernels: 0 us -> 39.4 us
  other arithmetic: 30.5 us -> 0 us
  local copies, waits for them, and re-layouts: 30.1 us -> 4.22 us
  starting transfers between devices: 15.8 us -> 0 us
  waiting for transfers between devices: 3.71 us -> 0 us
    dot_general x6 -> x0, matrix products: 41.8 us -> none  [the longest x3 23.2 us: attend_block(): jnp.einsum('hgqk,hkd->hgqd', weights.astype(jnp.bfloat16), value_rows, pr...]
    pallas_call x0 -> x1, Pallas kernels: none -> 39.4 us  [body(): pl.pallas_call(functools.partial(kernel, groups, prefix_levels), out_shap...]
    reduce_sum x3 -> x0, other arithmetic: 21.1 us -> none  [attend_block(): weight_sum = weight_sum * factor + jnp.sum(weights, axis=-1)]
    all_to_all x3 -> x0, starting transfers between devices: 15.8 us -> none  [the longest x1 6.35 us: body(): lax.all_to_all(first_send, 'pool', split_axis=2, concat_axis=2, tiled=True)]
    slice x6 -> x0, local copies, waits for them, and re-layouts: 10 us -> none  [the longest x4 7.37 us: block_step(): block_pages[1]]
    select_n x6 -> x0, other arithmetic: 6.75 us -> none  [the longest x2 2.86 us: level_rows(): return jnp.take(pool_kv, chosen, axis=2)]
    gather x4 -> x0, local copies, waits for them, and re-layouts: 5.17 us -> none  [the longest x1 2.48 us: body(): picked = jnp.take(own_pages, jnp.minimum(offset, suffix_pages - 1), axis=2)]
    all_to_all x3 -> x0, waiting for transfers between devices: 3.71 us -> none  [the longest x1 3.7 us: body(): lax.all_to_all(level_rows(begin_level, end_level), 'pool', split_axis=2,...]
  transfers between devices with their start and end apart: 3 -> 0, of which waited for: 1 -> 0; matrix products, arithmetic and copies ran while one was open for 79% -> 0% of each run, Pallas kernels for 0% -> 0%
where the time goes in v1:
time: 44.4 us; the launch traced here: 44.3 us
  Pallas kernels  39.4 us (89%)
  local copies, waits for them, and re-layouts  4.22 us (10%)
  between operations  0.65 us (1%)
    pallas_call x1, Pallas kernels, body(): pl.pallas_call(functools.partial(kernel, groups, prefix_levels), out_shap...  39.4 us
    unnamed x4, local copies, waits for them, and re-layouts  4.22 us

profile of v1, /device:TPU:0, one launch (start us, length us, event | category | flops | bytes accessed | tf_op | source)
XLA Modules:
  0.0 44.3 jit_solution(820419493111349482)
XLA Ops:
  0.6 39.4 %shard_map.77 = (bf16[512,2048]{1,0:T(8,128)(2,1)}, bf16[2,2,8,128,128]{4,3,2,1,0:T(8,128)(2,1)}) custom-call(s32[4]{0:T(128)} %length_ref.1, s32[4]{0:T(128)} %start_ref.1, s32[4,2,4]{2,1,0:T(2,128)} %bitcast.3, bf16[512,2048]{1,0:T(8,128)(2,1)} %q_ref.1, bf16[2,2,4,128,128]{4,3,2,1,0:T(8,128)(2,1)} %bitcast.2, bf16[2,2,8,128,128]{4,3,2,1,0:T(8,128)(2,1)} %pool_ref.1), custom_call_target="tpu_custom_call" | custom-call | tf_op jit(solution)/shard_map/pallas_call | solution.py:242
  40.0 0.0 copy-start
  40.0 3.2 %copy.10 = bf16[512,2048]{1,0:T(8,128)(2,1)} copy(bf16[512,2048]{1,0:T(8,128)(2,1)} %get-tuple-element.4) | data formatting | bytes 4194304
  43.3 0.0 copy-done
  43.3 1.0 %copy.11 = bf16[2,2,8,128,128]{4,3,2,1,0:T(8,128)(2,1)} copy(bf16[2,2,8,128,128]{4,3,2,1,0:T(8,128)(2,1)S(1)} %copy-done) | data formatting | bytes 2097152
Async XLA Ops:
  40.0 3.3 %copy-start = (bf16[2,2,8,128,128]{4,3,2,1,0:T(8,128)(2,1)S(1)}, bf16[2,2,8,128,128]{4,3,2,1,0:T(8,128)(2,1)}, u32[]{:S(2)}) copy-start(bf16[2,2,8,128,128]{4,3,2,1,0:T(8,128)(2,1)} %get-tuple-element.5) | copy-start | bytes 3145732

commit v2 on v1

--- a/solution.py
+++ b/solution.py
@@ -9,7 +9,7 @@
 from jax.sharding import PartitionSpec as P
 
 NT = (((1,), (1,)), ((), ()))
-ROWS = 128
+ROWS = 256
 KEY_BLOCK = 512
 
 
@@ -101,6 +101,44 @@
             )
             copy.start()
             copies.append(copy)
+    masks = {}
+    for at in range(0, rows, dim):
+        masks[at] = lax.broadcasted_iota(jnp.int32, (rows, dim), 1) + at <= lax.broadcasted_iota(
+            jnp.int32, (rows, dim), 0
+        )
+
+    def own_step(head, carry):
+        kv_head = head // per_kv
+        columns = pl.ds(pl.multiple_of(head * dim, dim), dim)
+        for first in range(0, suffix, rows):
+            end = first + rows
+            scores = lax.dot_general(
+                q_ref[first:end, columns],
+                own_ref[0, kv_head, : end // page_len].reshape(end, dim),
+                NT,
+                preferred_element_type=jnp.float32,
+            )
+            pieces = []
+            for at in range(0, end, dim):
+                piece = scores[:, at : at + dim]
+                if at + dim > first + 1:
+                    piece = jnp.where(masks[at - first], piece, -jnp.inf)
+                pieces.append(piece)
+            peak = functools.reduce(jnp.maximum, pieces)
+            highest = jnp.broadcast_to(jnp.max(peak, axis=1, keepdims=True), (rows, dim))
+            weights = jnp.concatenate(
+                [jnp.exp2((piece - highest) * factor).astype(jnp.bfloat16) for piece in pieces], axis=1
+            )
+            acc[head, first:end] = jnp.dot(
+                weights, own_values[kv_head, :end], preferred_element_type=jnp.float32
+            )
+            top[head, first:end] = highest
+        return carry
+
+    lax.fori_loop(0, heads, own_step, 0, unroll=4)
+
+    for copy in copies:
+        copy.wait()
     for step in range(1, groups):
         copy = pltpu.make_async_remote_copy(
             src_ref=back_send.at[step],
@@ -112,36 +150,6 @@
         )
         copy.start()
         back_copies.append(copy)
-
-    causal = lax.broadcasted_iota(jnp.int32, (rows, rows), 1) <= lax.broadcasted_iota(
-        jnp.int32, (rows, rows), 0
-    )
-
-    def own_step(head, carry):
-        kv_head = head // per_kv
-        columns = pl.ds(pl.multiple_of(head * dim, dim), dim)
-        for first in range(0, suffix, rows):
-            end = first + rows
-            scores = lax.dot_general(
-                q_ref[first:end, columns],
-                own_ref[0, kv_head, : end // page_len].reshape(end, dim),
-                NT,
-                preferred_element_type=jnp.float32,
-            )
-            last = jnp.where(causal, scores[:, first:], -jnp.inf)
-            scores = jnp.concatenate([scores[:, :first], last], axis=1) if first else last
-            highest = jnp.max(scores, axis=1, keepdims=True)
-            weights = jnp.exp2((scores - highest) * factor).astype(jnp.bfloat16)
-            acc[head, first:end] = jnp.dot(
-                weights, own_values[kv_head, :end], preferred_element_type=jnp.float32
-            )
-            top[head, first:end] = jnp.broadcast_to(highest, (rows, dim))
-        return carry
-
-    lax.fori_loop(0, heads, own_step, 0)
-
-    for copy in copies:
-        copy.wait()
     first_page = wrap(me - my_start)
     for level in range(prefix_levels):
         for step in range(groups):
@@ -196,7 +204,7 @@
             out_ref[first:end, columns] = (mixed[:, :dim] / mixed[:, dim:]).astype(jnp.bfloat16)
         return carry
 
-    lax.fori_loop(0, heads, page_step, 0)
+    lax.fori_loop(0, heads, page_step, 0, unroll=4)
 
     for copy in back_copies:
         copy.wait()

time: 44.4 us -> 36.3 us (0.82)
  Pallas kernels: 39.4 us -> 31.2 us
    pallas_call x1, Pallas kernels: 39.4 us -> 31.2 us  [body(): pl.pallas_call(functools.partial(kernel, groups, prefix_levels), out_shap...]
where the time goes in v2:
time: 36.3 us; the launch traced here: 36 us
  Pallas kernels  31.2 us (86%)
  local copies, waits for them, and re-layouts  4.22 us (12%)
  between operations  0.65 us (2%)
    pallas_call x1, Pallas kernels, body(): pl.pallas_call(functools.partial(kernel, groups, prefix_levels), out_shap...  31.2 us
    unnamed x4, local copies, waits for them, and re-layouts  4.22 us

profile of v2, /device:TPU:0, one launch (start us, length us, event | category | flops | bytes accessed | tf_op | source)
XLA Modules:
  0.0 36.0 jit_solution(7776658735251921562)
XLA Ops:
  0.6 31.2 %shard_map.77 = (bf16[512,2048]{1,0:T(8,128)(2,1)}, bf16[2,2,8,128,128]{4,3,2,1,0:T(8,128)(2,1)}) custom-call(s32[4]{0:T(128)} %length_ref.1, s32[4]{0:T(128)} %start_ref.1, s32[4,2,4]{2,1,0:T(2,128)} %bitcast.3, bf16[512,2048]{1,0:T(8,128)(2,1)} %q_ref.1, bf16[2,2,4,128,128]{4,3,2,1,0:T(8,128)(2,1)} %bitcast.2, bf16[2,2,8,128,128]{4,3,2,1,0:T(8,128)(2,1)} %pool_ref.1), custom_call_target="tpu_custom_call" | custom-call | tf_op jit(solution)/shard_map/pallas_call | solution.py:250
  31.8 0.0 copy-start
  31.8 3.2 %copy.10 = bf16[512,2048]{1,0:T(8,128)(2,1)} copy(bf16[512,2048]{1,0:T(8,128)(2,1)} %get-tuple-element.4) | data formatting | bytes 4194304
  35.1 0.0 copy-done
  35.1 1.0 %copy.11 = bf16[2,2,8,128,128]{4,3,2,1,0:T(8,128)(2,1)} copy(bf16[2,2,8,128,128]{4,3,2,1,0:T(8,128)(2,1)S(1)} %copy-done) | data formatting | bytes 2097152
Async XLA Ops:
  31.8 3.3 %copy-start = (bf16[2,2,8,128,128]{4,3,2,1,0:T(8,128)(2,1)S(1)}, bf16[2,2,8,128,128]{4,3,2,1,0:T(8,128)(2,1)}, u32[]{:S(2)}) copy-start(bf16[2,2,8,128,128]{4,3,2,1,0:T(8,128)(2,1)} %get-tuple-element.5) | copy-start | bytes 3145732

commit v3 on v2

--- a/solution.py
+++ b/solution.py
@@ -19,15 +19,18 @@
     length_ref,
     start_ref,
     slot_ref,
-    q_ref,
+    q_hbm,
     own_ref,
     pool_ref,
+    out_hbm,
+    back_recv,
+    q_ref,
     out_ref,
-    new_ref,
+    q_sem,
+    out_sem,
     send,
     recv,
     back_send,
-    back_recv,
     own_values,
     page_keys,
     page_values,
@@ -38,6 +41,8 @@
     back_send_sem,
     back_recv_sem,
 ):
+    q_load = pltpu.make_async_copy(q_hbm, q_ref, q_sem)
+    q_load.start()
     me = lax.axis_index("pool")
     local_heads = pool_ref.shape[1]
     slot_count = pool_ref.shape[2]
@@ -135,6 +140,7 @@
             top[head, first:end] = highest
         return carry
 
+    q_load.wait()
     lax.fori_loop(0, heads, own_step, 0, unroll=4)
 
     for copy in copies:
@@ -161,15 +167,17 @@
             span = slice(place * page_len, (place + 1) * page_len)
             for head in range(local_heads):
                 page_keys[head, span] = recv[source, 0, head]
-                page_values[head, span, :dim] = (
-                    recv[place, 1, head].astype(jnp.float32) * keep
-                ).astype(jnp.bfloat16)
+                page_values[head, span, :dim] = recv[place, 1, head] * keep.astype(jnp.bfloat16)
                 page_values[head, span, dim:] = jnp.full(
                     (page_len, dim), keep, jnp.float32
                 ).astype(jnp.bfloat16)
 
     total = prefix_levels * groups * page_len
     block = min(KEY_BLOCK, total)
+
+    def store(head):
+        columns = pl.ds(pl.multiple_of(head * dim, dim), dim)
+        return pltpu.make_async_copy(out_ref.at[head], out_hbm.at[:, columns], out_sem.at[head])
 
     def page_step(head, carry):
         kv_head = head // per_kv
@@ -201,37 +209,84 @@
                     preferred_element_type=jnp.float32,
                 )
                 highest = risen
-            out_ref[first:end, columns] = (mixed[:, :dim] / mixed[:, dim:]).astype(jnp.bfloat16)
+            out_ref[head, first:end] = (mixed[:, :dim] / mixed[:, dim:]).astype(jnp.bfloat16)
+        store(head).start()
         return carry
 
     lax.fori_loop(0, heads, page_step, 0, unroll=4)
 
+    def store_done(head, carry):
+        store(head).wait()
+        return carry
+
+    lax.fori_loop(0, heads, store_done, 0)
     for copy in back_copies:
         copy.wait()
+
+
+def finish(
+    groups,
+    length_ref,
+    start_ref,
+    slot_ref,
+    mixed_ref,
+    fresh_ref,
+    pool_ref,
+    out_ref,
+    new_ref,
+    mixed_buf,
+    page_buf,
+    mixed_in,
+    mixed_out,
+    page_in,
+    page_out,
+):
+    me = lax.axis_index("pool")
+    levels = slot_ref.shape[1]
+    slot_count = pool_ref.shape[2]
+    page_len = pool_ref.shape[3]
+    suffix_pages = mixed_ref.shape[0] // page_len
+    loads = []
+    for part in range(suffix_pages):
+        span = pl.ds(part * page_len, page_len)
+        load = pltpu.make_async_copy(mixed_ref.at[span], mixed_buf.at[span], mixed_in.at[part])
+        load.start()
+        loads.append(load)
     targets = []
     for step in range(groups):
         request = lax.rem(me - step + groups, groups)
-        offset = wrap(me - start_ref[request] - length_ref[request])
-        level = jnp.minimum((length_ref[request] + offset) // groups, levels - 1)
+        length = length_ref[request]
+        offset = lax.rem(me - start_ref[request] - length + groups * (levels + 1), groups)
+        level = jnp.minimum((length + offset) // groups, levels - 1)
         target = slot_ref[request, level, me]
         targets.append(jnp.where(offset < suffix_pages, target, slot_count))
-
-    def slot_step(slot, carry):
+    page_loads = []
+    for slot in range(slot_count):
         chosen = jnp.int32(0)
         hit = jnp.int32(0)
         for step in range(groups):
             match = targets[step] == slot
             chosen = jnp.where(match, step, chosen)
             hit = jnp.where(match, 1, hit)
-        taken = jnp.full((page_len, dim), hit, jnp.int32) > 0
-        for which in range(2):
-            for head in range(local_heads):
-                fresh = back_recv[chosen, which, head].astype(jnp.float32)
-                old = pool_ref[which, head, slot].astype(jnp.float32)
-                new_ref[which, head, slot] = jnp.where(taken, fresh, old).astype(jnp.bfloat16)
-        return carry
-
-    lax.fori_loop(0, slot_count, slot_step, 0)
+        keep = pltpu.make_async_copy(pool_ref.at[:, :, slot], page_buf.at[slot], page_in.at[slot])
+        swap = pltpu.make_async_copy(fresh_ref.at[chosen], page_buf.at[slot], page_in.at[slot])
+        pl.when(hit == 0)(keep.start)
+        pl.when(hit == 1)(swap.start)
+        page_loads.append(keep)
+    stores = []
+    for part, load in enumerate(loads):
+        load.wait()
+        span = pl.ds(part * page_len, page_len)
+        store = pltpu.make_async_copy(mixed_buf.at[span], out_ref.at[span], mixed_out.at[part])
+        store.start()
+        stores.append(store)
+    for slot, load in enumerate(page_loads):
+        load.wait()
+        store = pltpu.make_async_copy(page_buf.at[slot], new_ref.at[:, :, slot], page_out.at[slot])
+        store.start()
+        stores.append(store)
+    for store in stores:
+        store.wait()
 
 
 def body(queries, suffix_kv, pool_kv, prefix_pages, owner_start, page_slot):
@@ -247,18 +302,23 @@
     smem = pl.BlockSpec(memory_space=pltpu.SMEM)
     vmem = pl.BlockSpec(memory_space=pltpu.VMEM)
     bf16 = jnp.bfloat16
-    return pl.pallas_call(
+    anywhere = pl.BlockSpec(memory_space=pl.ANY)
+    slots = jnp.transpose(page_slot, (0, 2, 1))
+    mixed, fresh = pl.pallas_call(
         functools.partial(kernel, groups, prefix_levels),
         out_shape=(
             jax.ShapeDtypeStruct(queries.shape, bf16),
-            jax.ShapeDtypeStruct(pool_kv.shape, bf16),
+            jax.ShapeDtypeStruct((groups,) + page_shape, bf16),
         ),
-        in_specs=[smem, smem, smem, vmem, vmem, vmem],
-        out_specs=(vmem, vmem),
+        in_specs=[smem, smem, smem, anywhere, vmem, vmem],
+        out_specs=(anywhere, vmem),
         scratch_shapes=[
+            pltpu.VMEM(queries.shape, bf16),
+            pltpu.VMEM((heads, suffix, dim), bf16),
+            pltpu.SemaphoreType.DMA,
+            pltpu.SemaphoreType.DMA((heads,)),
             pltpu.VMEM((pages,) + page_shape, bf16),
             pltpu.VMEM((pages,) + page_shape, bf16),
-            pltpu.VMEM((groups,) + page_shape, bf16),
             pltpu.VMEM((groups,) + page_shape, bf16),
             pltpu.VMEM((local_heads, suffix, 2 * dim), bf16),
             pltpu.VMEM((local_heads, pages * page_len, dim), bf16),
@@ -271,16 +331,34 @@
             pltpu.SemaphoreType.DMA((groups,)),
         ],
         compiler_params=pltpu.CompilerParams(
-            collective_id=0, has_side_effects=True, vmem_limit_bytes=56 * 1024 * 1024
+            collective_id=0, has_side_effects=True, vmem_limit_bytes=60 * 1024 * 1024
         ),
     )(
         prefix_pages,
         owner_start,
-        jnp.transpose(page_slot, (0, 2, 1)),
+        slots,
         queries,
         suffix_kv.reshape(2, local_heads, suffix_pages, page_len, dim),
         pool_kv,
     )
+    return pl.pallas_call(
+        functools.partial(finish, groups),
+        out_shape=(
+            jax.ShapeDtypeStruct(queries.shape, bf16),
+            jax.ShapeDtypeStruct(pool_kv.shape, bf16),
+        ),
+        in_specs=[smem, smem, smem, anywhere, anywhere, anywhere],
+        out_specs=(anywhere, anywhere),
+        scratch_shapes=[
+            pltpu.VMEM(queries.shape, bf16),
+            pltpu.VMEM((slot_count,) + page_shape, bf16),
+            pltpu.SemaphoreType.DMA((suffix_pages,)),
+            pltpu.SemaphoreType.DMA((suffix_pages,)),
+            pltpu.SemaphoreType.DMA((slot_count,)),
+            pltpu.SemaphoreType.DMA((slot_count,)),
+        ],
+        compiler_params=pltpu.CompilerParams(vmem_limit_bytes=60 * 1024 * 1024),
+    )(prefix_pages, owner_start, slots, mixed, fresh, pool_kv)
 
 
 def solution(mesh):

time: 36.3 us -> 34.6 us (0.953)
  local copies, waits for them, and re-layouts: 4.22 us -> 0 us
  Pallas kernels: 31.2 us -> 33.6 us
    unnamed x4 -> x0, local copies, waits for them, and re-layouts: 4.22 us -> none
    pallas_call x0 -> x1, Pallas kernels: none -> 4.07 us  [body(): pl.pallas_call(functools.partial(finish, groups), out_shape=(jax.ShapeDty...]
    pallas_call x1, Pallas kernels: 31.2 us -> 29.6 us  [body(): pl.pallas_call(functools.partial(kernel, groups, prefix_levels), out_shap...]
where the time goes in v3:
time: 34.6 us; the launch traced here: 34.3 us
  Pallas kernels  33.6 us (97%)
  between operations  0.64 us (2%)
    pallas_call x1, Pallas kernels, body(): pl.pallas_call(functools.partial(kernel, groups, prefix_levels), out_shap...  29.6 us
    pallas_call x1, Pallas kernels, body(): pl.pallas_call(functools.partial(finish, groups), out_shape=(jax.ShapeDty...  4.07 us

profile of v3, /device:TPU:0, one launch (start us, length us, event | category | flops | bytes accessed | tf_op | source)
XLA Modules:
  0.0 34.3 jit_solution(8721360081837309190)
XLA Ops:
  0.6 29.6 %shard_map.77 = (bf16[512,2048]{1,0:T(8,128)(2,1)}, bf16[4,2,2,128,128]{4,3,2,1,0:T(8,128)(2,1)}) custom-call(s32[4]{0:T(128)} %length_ref.3, s32[4]{0:T(128)} %start_ref.3, s32[4,2,4]{2,1,0:T(2,128)} %bitcast.3, bf16[512,2048]{1,0:T(8,128)(2,1)} %q_hbm.1, bf16[2,2,4,128,128]{4,3,2,1,0:T(8,128)(2,1)} %bitcast.2, bf16[2,2,8,128,128]{4,3,2,1,0:T(8,128)(2,1)} %pool_ref.3), custom_call_target="tpu_custom_call" | custom-call | tf_op jit(solution)/shard_map/pallas_call | solution.py:307
  30.2 4.1 %shard_map.78 = (bf16[512,2048]{1,0:T(8,128)(2,1)}, bf16[2,2,8,128,128]{4,3,2,1,0:T(8,128)(2,1)}) custom-call(s32[4]{0:T(128)} %length_ref.3, s32[4]{0:T(128)} %start_ref.3, s32[4,2,4]{2,1,0:T(2,128)} %bitcast.4, bf16[512,2048]{1,0:T(8,128)(2,1)} %get-tuple-element.4.mixed_ref, bf16[4,2,2,128,128]{4,3,2,1,0:T(8,128)(2,1)} %get-tuple-element.5.fresh_ref, ...), custom_call_target="tpu_custom_call" | custom-call | tf_op jit(solution)/shard_map/pallas_call | solution.py:344
